TPU v7x, 32 devices: a whole 2x2x4 slice. The times are simulated.
32 devices in a mesh: dp: 2 (over core), block: 16 (over z, y, x).
Axes of the slice: x: 2, y: 2, z: 4, core: 2. Of those that a mesh axis runs over, the one named last changes fastest.
Arguments:
- inputs: bfloat16 [8192, 2048], P('block', 'dp'), may hold values from -6 to 6
- grad_out: bfloat16 [8192, 2048], P('block', 'dp'), may hold values from -6 to 6
- right_first: bfloat16 [64, 128, 128], P('block'), may hold values from -0.5 to 0.5
- left_first: bfloat16 [128, 64, 64], P('block'), may hold values from -0.75 to 0.75
- right_gate: bfloat16 [64, 128, 128], P('block'), may hold values from -0.5 to 0.5
- left_gate: bfloat16 [128, 64, 64], P('block'), may hold values from -0.75 to 0.75
- right_mix: bfloat16 [64, 128, 128], P('block'), may hold values from -0.5 to 0.5
- left_mix: bfloat16 [128, 64, 64], P('block'), may hold values from -0.75 to 0.75
Outputs:
- outputs: bfloat16 [8192, 2048], P('block', 'dp')
- grad_in: bfloat16 [8192, 2048], P('block', 'dp')
- grad_right_first: float32 [64, 128, 128], P('block', 'dp')
- grad_left_first: float32 [128, 64, 64], P('block', 'dp')
- grad_right_gate: float32 [64, 128, 128], P('block', 'dp')
- grad_left_gate: float32 [128, 64, 64], P('block', 'dp')
- grad_right_mix: float32 [64, 128, 128], P('block', 'dp')
- grad_left_mix: float32 [128, 64, 64], P('block', 'dp')
All inputs are finite; a program needn't handle non-finite values.
Results may differ from a plain program's by a relative error of at most 0.017.
Values may be sent and summed in bfloat16 or wider, within the bound.
A program may use at most 64 MiB of HBM per device.

v0:
```python
import jax
import jax.numpy as jnp
from jax import lax
from jax.sharding import PartitionSpec as P


def outgoing(weight, values, groups):
    shaped = values.reshape(weight.shape[0], weight.shape[2], -1)
    sectioned = jnp.einsum(
        "bik,bkt->bit", weight, shaped, preferred_element_type=jnp.float32
    ).astype(jnp.bfloat16)
    return sectioned.reshape(sectioned.shape[0], groups, -1, sectioned.shape[2])


def arrange(received):
    return received.reshape(-1, received.shape[2], received.shape[3])


def combine(weight, arranged):
    return jnp.einsum("jks,sjt->jkt", weight, arranged, preferred_element_type=jnp.float32)


def left_grads(weight, arranged, grad_rows, groups):
    grad_weight = jnp.einsum(
        "jkt,sjt->jks", grad_rows, arranged, preferred_element_type=jnp.float32
    )
    split_weight = weight.reshape(weight.shape[0], weight.shape[1], groups, -1)
    back_rows = jnp.einsum(
        "jkcr,jkt->rcjt", split_weight, grad_rows, preferred_element_type=jnp.float32
    )
    return (grad_weight, back_rows.astype(jnp.bfloat16))


def right_grads(weight, back_rows, values):
    shaped = values.reshape(weight.shape[0], weight.shape[2], -1)
    grad_weight = jnp.einsum("bit,bkt->bik", back_rows, shaped, preferred_element_type=jnp.float32)
    through = jnp.einsum("bik,bit->bkt", weight, back_rows, preferred_element_type=jnp.float32)
    return (grad_weight, through.reshape(-1, through.shape[2]))


def shards(inputs, grad_out, right_first, left_first, right_gate, left_gate, right_mix, left_mix):
    groups = lax.axis_size("block")
    rows, count = inputs.shape
    send_first = outgoing(right_first, inputs, groups)
    send_gate = outgoing(right_gate, inputs, groups)
    sectioned_first = arrange(
        lax.all_to_all(send_first, "block", split_axis=1, concat_axis=0, tiled=True)
    )
    sectioned_gate = arrange(
        lax.all_to_all(send_gate, "block", split_axis=1, concat_axis=0, tiled=True)
    )
    first_results = (
        combine(left_first, sectioned_first),
        combine(left_gate, sectioned_gate),
        sectioned_first,
        sectioned_gate,
    )
    value_parts = first_results[0]
    gate_parts = first_results[1]
    sectioned_first = first_results[2]
    sectioned_gate = first_results[3]
    value = value_parts.reshape(rows, count)
    gate = gate_parts.reshape(rows, count)
    sigma = jax.nn.sigmoid(gate)
    hidden = (value * gate * sigma).astype(jnp.bfloat16)
    send_mix = outgoing(right_mix, hidden, groups)
    sectioned = arrange(lax.all_to_all(send_mix, "block", split_axis=1, concat_axis=0, tiled=True))
    mixed_parts = combine(left_mix, sectioned)
    outputs = (inputs.astype(jnp.float32) + mixed_parts.reshape(rows, count)).astype(jnp.bfloat16)
    grad_rows = grad_out.reshape(left_mix.shape[0], left_mix.shape[1], count)
    grad_left_mix, back_mix = left_grads(left_mix, sectioned, grad_rows, groups)
    back_mix = lax.all_to_all(back_mix, "block", split_axis=1, concat_axis=1, tiled=True)
    back_mix = back_mix.reshape(right_mix.shape[0], right_mix.shape[1], count)
    grad_right_mix, grad_hidden = right_grads(right_mix, back_mix, hidden)
    grad_value = (grad_hidden * gate * sigma).astype(jnp.bfloat16)
    grad_gate = (grad_hidden * value * sigma * (1.0 + gate * (1.0 - sigma))).astype(jnp.bfloat16)
    value_rows = grad_value.reshape(left_first.shape[0], left_first.shape[1], count)
    gate_grad_rows = grad_gate.reshape(left_gate.shape[0], left_gate.shape[1], count)
    grad_left_first, back_first = left_grads(left_first, sectioned_first, value_rows, groups)
    grad_left_gate, back_gate = left_grads(left_gate, sectioned_gate, gate_grad_rows, groups)
    back_first, back_gate = (
        lax.all_to_all(back_first, "block", split_axis=1, concat_axis=1, tiled=True),
        lax.all_to_all(back_gate, "block", split_axis=1, concat_axis=1, tiled=True),
    )
    back_first = back_first.reshape(right_first.shape[0], right_first.shape[1], count)
    back_gate = back_gate.reshape(right_gate.shape[0], right_gate.shape[1], count)
    grad_right_first, through_first = right_grads(right_first, back_first, inputs)
    grad_right_gate, through_gate = right_grads(right_gate, back_gate, inputs)
    grad_in = (grad_out.astype(jnp.float32) + through_first + through_gate).astype(jnp.bfloat16)
    (
        summed_right_first,
        summed_left_first,
        summed_right_gate,
        summed_left_gate,
        summed_right_mix,
        summed_left_mix,
    ) = (
        lax.psum_scatter(
            grad_right_first.astype(jnp.bfloat16), "dp", scatter_dimension=1, tiled=True
        ).astype(jnp.float32),
        lax.psum_scatter(
            grad_left_first.astype(jnp.bfloat16), "dp", scatter_dimension=1, tiled=True
        ).astype(jnp.float32),
        lax.psum_scatter(
            grad_right_gate.astype(jnp.bfloat16), "dp", scatter_dimension=1, tiled=True
        ).astype(jnp.float32),
        lax.psum_scatter(
            grad_left_gate.astype(jnp.bfloat16), "dp", scatter_dimension=1, tiled=True
        ).astype(jnp.float32),
        lax.psum_scatter(
            grad_right_mix.astype(jnp.bfloat16), "dp", scatter_dimension=1, tiled=True
        ).astype(jnp.float32),
        lax.psum_scatter(
            grad_left_mix.astype(jnp.bfloat16), "dp", scatter_dimension=1, tiled=True
        ).astype(jnp.float32),
    )
    return (
        outputs,
        grad_in,
        summed_right_first,
        summed_left_first,
        summed_right_gate,
        summed_left_gate,
        summed_right_mix,
        summed_left_mix,
    )


def solution(mesh):
    return jax.shard_map(
        shards,
        mesh=mesh,
        in_specs=(
            P("block", "dp"),
            P("block", "dp"),
            P("block", None, None),
            P("block", None, None),
            P("block", None, None),
            P("block", None, None),
            P("block", None, None),
            P("block", None, None),
        ),
        out_specs=(
            P("block", "dp"),
            P("block", "dp"),
            P("block", "dp", None),
            P("block", "dp", None),
            P("block", "dp", None),
            P("block", "dp", None),
            P("block", "dp", None),
            P("block", "dp", None),
        ),
        check_vma=False,
    )
```

profile of v0, /device:TPU:15, one launch (start us, length us, event | category | flops | bytes accessed | tf_op | source)
XLA Modules:
  0.0 253.9 jit_solution(9005996735255004403)
XLA Ops:
  11.7 6.6 %all-to-all-start.3 = ((bf16[4,16,8,1024]{3,0,2,1:T(4,128)(2,1)}), bf16[4,16,8,1024]{3,0,2,1:T(4,128)(2,1)S(1)}, u32[]{:S(2)}, u32[]{:S(2)}) async-start(bf16[4,16,8,1024]{3,0,2,1:T(4,128)(2,1)} %copy.50), calls=%async_computation.3 | async-start | bytes 2097152 | tf_op jit(solution)/shard_map/all_to_all | solution.py:72
  19.8 22.4 %all-to-all-done.3 = bf16[4,16,8,1024]{3,0,2,1:T(4,128)(2,1)S(1)} async-done(((bf16[4,16,8,1024]{3,0,2,1:T(4,128)(2,1)}), bf16[4,16,8,1024]{3,0,2,1:T(4,128)(2,1)S(1)}, u32[]{:S(2)}, u32[]{:S(2)}) %all-to-all-start.3) | async-done | bytes 1048608 | tf_op jit(solution)/shard_map/all_to_all | solution.py:72
  42.2 4.9 %all-to-all-start = ((bf16[4,16,8,1024]{3,2,0,1:T(8,128)(2,1)}), bf16[4,16,8,1024]{3,2,0,1:T(8,128)(2,1)S(1)}, u32[]{:S(2)}, u32[]{:S(2)}) async-start(bf16[4,16,8,1024]{3,2,0,1:T(8,128)(2,1)} %copy.42), calls=%async_computation | async-start | bytes 2097152 | tf_op jit(solution)/shard_map/all_to_all | solution.py:47
  48.6 22.4 %all-to-all-done = bf16[4,16,8,1024]{3,2,0,1:T(8,128)(2,1)S(1)} async-done(((bf16[4,16,8,1024]{3,2,0,1:T(8,128)(2,1)}), bf16[4,16,8,1024]{3,2,0,1:T(8,128)(2,1)S(1)}, u32[]{:S(2)}, u32[]{:S(2)}) %all-to-all-start) | async-done | bytes 1048608 | tf_op jit(solution)/shard_map/all_to_all | solution.py:47
  71.0 5.0 %all-to-all-start.1 = ((bf16[4,16,8,1024]{3,2,0,1:T(8,128)(2,1)}), bf16[4,16,8,1024]{3,2,0,1:T(8,128)(2,1)}, u32[]{:S(2)}, u32[]{:S(2)}) async-start(bf16[4,16,8,1024]{3,2,0,1:T(8,128)(2,1)} %copy.44), calls=%async_computation.1 | async-start | bytes 2097152 | tf_op jit(solution)/shard_map/all_to_all | solution.py:50
  76.0 3.7 %fusion.38 = f32[8,1024,64]{1,2,0:T(8,128)} fusion(bf16[8,64,64]{2,1,0:T(8,128)(2,1)} %param.11, bf16[64,8,1024]{2,1,0:T(8,128)(2,1)S(1)} %bitcast.150), kind=kOutput, calls=%fused_computation.58 | convolution fusion | flops 67108864 | bytes 3211264 | tf_op jit(solution)/shard_map/jks,sjt->jkt/dot_general | solution.py:20
  81.9 18.1 %all-to-all-done.1 = bf16[4,16,8,1024]{3,2,0,1:T(8,128)(2,1)} async-done(((bf16[4,16,8,1024]{3,2,0,1:T(8,128)(2,1)}), bf16[4,16,8,1024]{3,2,0,1:T(8,128)(2,1)}, u32[]{:S(2)}, u32[]{:S(2)}) %all-to-all-start.1) | async-done | bytes 1048608 | tf_op jit(solution)/shard_map/all_to_all | solution.py:50
  100.0 5.8 %fusion.8 = (bf16[8,64,1024]{2,1,0:T(8,128)(2,1)S(1)}, bf16[8,64,1024]{2,1,0:T(8,128)(2,1)}, bf16[8,64,1024]{2,1,0:T(8,128)(2,1)S(1)}) fusion(f32[8,64,1024]{2,1,0:T(8,128)} %bitcast.154, f32[8,1024,64]{1,2,0:T(8,128)} %fusion.38, bf16[8,64,64]{2,1,0:T(8,128)(2,1)} %param.13, bf16[64,8,1024]{2,1,0:T(8,128)(2,1)} %bitcast.9), kind=kOutput, calls=%fused_computation.15 | convolution fusion | flops 75497472 | bytes 8454144 | tf_op jit(solution)/shard_map/jks,sjt->jkt/dot_general | solution.py:20
  108.2 5.0 %all-to-all-start.2 = ((bf16[4,16,8,1024]{3,2,0,1:T(8,128)(2,1)}), bf16[4,16,8,1024]{3,2,0,1:T(8,128)(2,1)S(1)}, u32[]{:S(2)}, u32[]{:S(2)}) async-start(bf16[4,16,8,1024]{3,2,0,1:T(8,128)(2,1)} %copy.46), calls=%async_computation.2 | async-start | bytes 2097152 | tf_op jit(solution)/shard_map/all_to_all | solution.py:67
  118.0 19.0 %all-to-all-done.2 = bf16[4,16,8,1024]{3,2,0,1:T(8,128)(2,1)S(1)} async-done(((bf16[4,16,8,1024]{3,2,0,1:T(8,128)(2,1)}), bf16[4,16,8,1024]{3,2,0,1:T(8,128)(2,1)S(1)}, u32[]{:S(2)}, u32[]{:S(2)}) %all-to-all-start.2) | async-done | bytes 1048608 | tf_op jit(solution)/shard_map/all_to_all | solution.py:67
  137.1 5.0 %all-to-all-start.4 = ((bf16[4,16,8,1024]{3,0,2,1:T(4,128)(2,1)}), bf16[4,16,8,1024]{3,0,2,1:T(4,128)(2,1)S(1)}, u32[]{:S(2)}, u32[]{:S(2)}) async-start(bf16[4,16,8,1024]{3,0,2,1:T(4,128)(2,1)} %copy.55), calls=%async_computation.4 | async-start | bytes 2097152 | tf_op jit(solution)/shard_map/all_to_all | solution.py:82
  147.2 18.7 %all-to-all-done.4 = bf16[4,16,8,1024]{3,0,2,1:T(4,128)(2,1)S(1)} async-done(((bf16[4,16,8,1024]{3,0,2,1:T(4,128)(2,1)}), bf16[4,16,8,1024]{3,0,2,1:T(4,128)(2,1)S(1)}, u32[]{:S(2)}, u32[]{:S(2)}) %all-to-all-start.4) | async-done | bytes 1048608 | tf_op jit(solution)/shard_map/all_to_all | solution.py:82
  165.9 5.0 %all-to-all-start.5 = ((bf16[4,16,8,1024]{3,0,2,1:T(4,128)(2,1)}), bf16[4,16,8,1024]{3,0,2,1:T(4,128)(2,1)}, u32[]{:S(2)}, u32[]{:S(2)}) async-start(bf16[4,16,8,1024]{3,0,2,1:T(4,128)(2,1)} %copy.60), calls=%async_computation.5 | async-start | bytes 2097152 | tf_op jit(solution)/shard_map/all_to_all | solution.py:83
  171.2 3.0 %convolution_convert_fusion.8 = bf16[8,64,64]{2,1,0:T(8,128)(2,1)} fusion(bf16[8,64,1024]{2,1,0:T(8,128)(2,1)} %get-tuple-element.33, bf16[64,8,1024]{2,1,0:T(8,128)(2,1)} %bitcast.9), kind=kOutput, calls=%fused_computation.35 | convolution fusion | flops 67141632 | bytes 2162688 | tf_op jit(solution)/shard_map/jkt,sjt->jks/dot_general | solution.py:24
  174.3 3.0 %convolution_convert_fusion.10 = bf16[8,64,64]{2,1,0:T(8,128)(2,1)} fusion(bf16[8,64,1024]{2,1,0:T(8,128)(2,1)} %copy-done.9, bf16[64,8,1024]{2,1,0:T(8,128)(2,1)} %bitcast.151), kind=kOutput, calls=%fused_computation.37 | convolution fusion | flops 67141632 | bytes 2162688 | tf_op jit(solution)/shard_map/jkt,sjt->jks/dot_general | solution.py:24
  177.4 2.8 %convolution_convert_fusion.7 = bf16[4,128,128]{2,1,0:T(8,128)(2,1)} fusion(bf16[4,128,1024]{2,1,0:T(8,128)(2,1)} %bitcast.156, bf16[4,16,8,1024]{3,0,2,1:T(4,128)(2,1)} %copy-done.5), kind=kOutput, calls=%fused_computation.34 | convolution fusion | flops 134283264 | bytes 2228224 | tf_op jit(solution)/shard_map/bit,bkt->bik/dot_general | solution.py:36
  180.2 5.6 %reduce-scatter.13.cloned.1.call-done = bf16[8,32,64]{2,1,0:T(8,128)(2,1)} async-done(((bf16[8,64,64]{2,1,0:T(8,128)(2,1)}), bf16[8,32,64]{2,1,0:T(8,128)(2,1)}) %reduce-scatter.13.cloned.1.call-update) | async-done | bytes 32784 | tf_op jit(solution)/shard_map/reduce_scatter | solution.py:107
  187.3 10.0 %reduce-scatter.9.cloned.1.call-done = bf16[8,32,64]{2,1,0:T(8,128)(2,1)} async-done(((bf16[8,64,64]{2,1,0:T(8,128)(2,1)}), bf16[8,32,64]{2,1,0:T(8,128)(2,1)}) %reduce-scatter.9.cloned.1.call-update) | async-done | bytes 32784 | tf_op jit(solution)/shard_map/reduce_scatter | solution.py:101
  198.8 10.0 %reduce-scatter.15.cloned.1.call-done = bf16[4,64,128]{2,1,0:T(8,128)(2,1)} async-done(((bf16[4,128,128]{2,1,0:T(8,128)(2,1)}), bf16[4,64,128]{2,1,0:T(8,128)(2,1)}) %reduce-scatter.15.cloned.1.call-update) | async-done | bytes 65552 | tf_op jit(solution)/shard_map/reduce_scatter | solution.py:110
  210.3 2.7 %fusion.19 = bf16[8,64,64]{1,2,0:T(8,128)(2,1)} fusion(bf16[8,64,1024]{2,1,0:T(8,128)(2,1)} %bitcast.153, bf16[64,8,1024]{2,1,0:T(8,128)(2,1)S(1)} %bitcast.148), kind=kOutput, calls=%fused_computation.39 | convolution fusion | flops 67141632 | bytes 2162688 | tf_op jit(solution)/shard_map/jkt,sjt->jks/dot_general | solution.py:24
  216.0 2.8 %fusion.32 = f32[8,1024,64]{1,2,0:T(8,128)S(1)} fusion(bf16[8,64,64]{2,1,0:T(8,128)(2,1)} %param.15, bf16[64,8,1024]{2,1,0:T(8,128)(2,1)} %bitcast.149), kind=kOutput, calls=%fused_computation.52 | convolution fusion | flops 67108864 | bytes 3211264 | tf_op jit(solution)/shard_map/jks,sjt->jkt/dot_general | solution.py:20
  218.8 2.4 convolution_convert_fusion.9
  229.1 5.7 %reduce-scatter.7.cloned.1.call-done = bf16[4,64,128]{2,1,0:T(8,128)(2,1)} async-done(((bf16[4,128,128]{2,1,0:T(8,128)(2,1)}), bf16[4,64,128]{2,1,0:T(8,128)(2,1)}) %reduce-scatter.7.cloned.1.call-update) | async-done | bytes 65552 | tf_op jit(solution)/shard_map/reduce_scatter | solution.py:98
  236.3 9.2 %reduce-scatter.11.cloned.1.call-done = bf16[4,64,128]{2,1,0:T(8,128)(2,1)} async-done(((bf16[4,128,128]{2,1,0:T(8,128)(2,1)}), bf16[4,64,128]{2,1,0:T(8,128)(2,1)}) %reduce-scatter.11.cloned.1.call-update) | async-done | bytes 65552 | tf_op jit(solution)/shard_map/reduce_scatter | solution.py:104
  (66 shorter events, 40.9 us)
Async XLA Ops:
  7.2 72.5 %copy-start = (bf16[4,128,128]{2,1,0:T(8,128)(2,1)S(1)}, bf16[4,128,128]{2,1,0:T(8,128)(2,1)}, u32[]{:S(2)}) copy-start(bf16[4,128,128]{2,1,0:T(8,128)(2,1)} %param.14) | copy-start | bytes 393220
  9.9 8.4 %copy-start.1 = (bf16[512,1024]{1,0:T(8,128)(2,1)S(1)}, bf16[512,1024]{1,0:T(8,128)(2,1)}, u32[]{:S(2)}) copy-start(bf16[512,1024]{1,0:T(8,128)(2,1)} %param.8) | copy-start | bytes 3145732
  9.9 8.4 %copy-start.11 = (bf16[4,128,128]{2,1,0:T(8,128)(2,1)S(1)}, bf16[4,128,128]{2,1,0:T(8,128)(2,1)}, u32[]{:S(2)}) copy-start(bf16[4,128,128]{2,1,0:T(8,128)(2,1)} %param.10) | copy-start | bytes 393220
  11.7 30.5 %all-to-all-start.3 = ((bf16[4,16,8,1024]{3,0,2,1:T(4,128)(2,1)}), bf16[4,16,8,1024]{3,0,2,1:T(4,128)(2,1)S(1)}, u32[]{:S(2)}, u32[]{:S(2)}) async-start(bf16[4,16,8,1024]{3,0,2,1:T(4,128)(2,1)} %copy.50), calls=%async_computation.3 | async-start | bytes 2097152 | tf_op jit(solution)/shard_map/all_to_all | solution.py:72
  18.7 28.4 %copy-start.10 = (bf16[4,128,128]{2,1,0:T(8,128)(2,1)S(1)}, bf16[4,128,128]{2,1,0:T(8,128)(2,1)}, u32[]{:S(2)}) copy-start(bf16[4,128,128]{2,1,0:T(8,128)(2,1)} %param.12) | copy-start | bytes 393220
  42.2 37.4 %copy-start.5 = (bf16[4,16,8,1024]{3,0,2,1:T(4,128)(2,1)}, bf16[4,16,8,1024]{3,0,2,1:T(4,128)(2,1)S(1)}, u32[]{:S(2)}) copy-start(bf16[4,16,8,1024]{3,0,2,1:T(4,128)(2,1)S(1)} %all-to-all-done.3) | copy-start | bytes 3145732
  42.2 28.8 %all-to-all-start = ((bf16[4,16,8,1024]{3,2,0,1:T(8,128)(2,1)}), bf16[4,16,8,1024]{3,2,0,1:T(8,128)(2,1)S(1)}, u32[]{:S(2)}, u32[]{:S(2)}) async-start(bf16[4,16,8,1024]{3,2,0,1:T(8,128)(2,1)} %copy.42), calls=%async_computation | async-start | bytes 2097152 | tf_op jit(solution)/shard_map/all_to_all | solution.py:47
  71.0 8.7 %copy-start.6 = (bf16[4,16,8,1024]{3,2,0,1:T(8,128)(2,1)}, bf16[4,16,8,1024]{3,2,0,1:T(8,128)(2,1)S(1)}, u32[]{:S(2)}) copy-start(bf16[4,16,8,1024]{3,2,0,1:T(8,128)(2,1)S(1)} %all-to-all-done) | copy-start | bytes 3145732
  71.0 29.0 %all-to-all-start.1 = ((bf16[4,16,8,1024]{3,2,0,1:T(8,128)(2,1)}), bf16[4,16,8,1024]{3,2,0,1:T(8,128)(2,1)}, u32[]{:S(2)}, u32[]{:S(2)}) async-start(bf16[4,16,8,1024]{3,2,0,1:T(8,128)(2,1)} %copy.44), calls=%async_computation.1 | async-start | bytes 2097152 | tf_op jit(solution)/shard_map/all_to_all | solution.py:50
  105.7 1.0 copy-start.8
  105.7 9.1 %copy-start.9 = (bf16[8,64,1024]{2,1,0:T(8,128)(2,1)}, bf16[8,64,1024]{2,1,0:T(8,128)(2,1)S(1)}, u32[]{:S(2)}) copy-start(bf16[8,64,1024]{2,1,0:T(8,128)(2,1)S(1)} %get-tuple-element.32) | copy-start | bytes 3145732
  108.2 28.9 %all-to-all-start.2 = ((bf16[4,16,8,1024]{3,2,0,1:T(8,128)(2,1)}), bf16[4,16,8,1024]{3,2,0,1:T(8,128)(2,1)S(1)}, u32[]{:S(2)}, u32[]{:S(2)}) async-start(bf16[4,16,8,1024]{3,2,0,1:T(8,128)(2,1)} %copy.46), calls=%async_computation.2 | async-start | bytes 2097152 | tf_op jit(solution)/shard_map/all_to_all | solution.py:67
  137.1 73.2 %copy-start.4 = (bf16[4,16,8,1024]{3,2,0,1:T(8,128)(2,1)}, bf16[4,16,8,1024]{3,2,0,1:T(8,128)(2,1)S(1)}, u32[]{:S(2)}) copy-start(bf16[4,16,8,1024]{3,2,0,1:T(8,128)(2,1)S(1)} %all-to-all-done.2) | copy-start | bytes 3145732
  137.1 28.9 %all-to-all-start.4 = ((bf16[4,16,8,1024]{3,0,2,1:T(4,128)(2,1)}), bf16[4,16,8,1024]{3,0,2,1:T(4,128)(2,1)S(1)}, u32[]{:S(2)}, u32[]{:S(2)}) async-start(bf16[4,16,8,1024]{3,0,2,1:T(4,128)(2,1)} %copy.55), calls=%async_computation.4 | async-start | bytes 2097152 | tf_op jit(solution)/shard_map/all_to_all | solution.py:82
  165.9 48.8 %copy-start.2 = (bf16[4,16,8,1024]{3,0,2,1:T(4,128)(2,1)}, bf16[4,16,8,1024]{3,0,2,1:T(4,128)(2,1)S(1)}, u32[]{:S(2)}) copy-start(bf16[4,16,8,1024]{3,0,2,1:T(4,128)(2,1)S(1)} %all-to-all-done.4) | copy-start | bytes 3145732
  165.9 52.9 %all-to-all-start.5 = ((bf16[4,16,8,1024]{3,0,2,1:T(4,128)(2,1)}), bf16[4,16,8,1024]{3,0,2,1:T(4,128)(2,1)}, u32[]{:S(2)}, u32[]{:S(2)}) async-start(bf16[4,16,8,1024]{3,0,2,1:T(4,128)(2,1)} %copy.60), calls=%async_computation.5 | async-start | bytes 2097152 | tf_op jit(solution)/shard_map/all_to_all | solution.py:83
  171.0 14.8 %reduce-scatter.13.cloned.1.call-start = ((), (), s32[]{:S(2)}) async-start(), calls=%async_computation.15 | async-start | bytes 196608 | tf_op jit(solution)/shard_map/reduce_scatter | solution.py:107
  174.3 23.0 %reduce-scatter.9.cloned.1.call-start = ((), (), s32[]{:S(2)}) async-start(), calls=%async_computation.13 | async-start | bytes 196608 | tf_op jit(solution)/shard_map/reduce_scatter | solution.py:101
  177.4 31.4 %reduce-scatter.15.cloned.1.call-start = ((), (), s32[]{:S(2)}) async-start(), calls=%async_computation.16 | async-start | bytes 196608 | tf_op jit(solution)/shard_map/reduce_scatter | solution.py:110
  180.2 47.4 %reduce-scatter.17.cloned.1.call-start = ((), (), s32[]{:S(2)}) async-start(), calls=%async_computation.17 | async-start | bytes 196608 | tf_op jit(solution)/shard_map/reduce_scatter | solution.py:113
  214.7 20.1 %reduce-scatter.7.cloned.1.call-start = ((), (), s32[]{:S(2)}) async-start(), calls=%async_computation.12 | async-start | bytes 196608 | tf_op jit(solution)/shard_map/reduce_scatter | solution.py:98
  216.0 29.6 %reduce-scatter.11.cloned.1.call-start = ((), (), s32[]{:S(2)}) async-start(), calls=%async_computation.14 | async-start | bytes 196608 | tf_op jit(solution)/shard_map/reduce_scatter | solution.py:104
  221.3 2.2 copy-start.3
  223.5 1.2 copy-start.7
Sparse Core Ops, SparseCore 0:
  174.6 11.1 reduce-scatter.12
  188.6 8.6 reduce-scatter.8
  200.1 8.6 reduce-scatter.14
  214.8 8.6 reduce-scatter.16
  226.1 8.6 reduce-scatter.6
  236.9 8.6 reduce-scatter.10
where the time goes:
time: 256 us; the launch traced here: 254 us
  waiting for transfers between devices  141 us (55%)
  matrix products  38.6 us (15%)
  starting transfers between devices  31.9 us (12%)
  local copies, waits for them, and re-layouts  17.6 us (7%)
  between operations  14.3 us (6%)
  other arithmetic  10.4 us (4%)
    all_to_all x1, waiting for transfers between devices, shards(): lax.all_to_all(back_mix, 'block', split_axis=1, concat_axis=1, tiled=True)  22.4 us
    all_to_all x1, waiting for transfers between devices, shards(): lax.all_to_all(send_first, 'block', split_axis=1, concat_axis=0, tiled=True)  22.4 us
    all_to_all x1, waiting for transfers between devices, shards(): lax.all_to_all(send_mix, 'block', split_axis=1, concat_axis=0, tiled=True)  19 us
    all_to_all x1, waiting for transfers between devices, shards(): lax.all_to_all(back_first, 'block', split_axis=1, concat_axis=1, tiled=True)  18.7 us
    all_to_all x1, waiting for transfers between devices, shards(): lax.all_to_all(send_gate, 'block', split_axis=1, concat_axis=0, tiled=True)  18.1 us
    dot_general x3, matrix products, combine(): jnp.einsum('jks,sjt->jkt', weight, arranged, preferred_element_type=jnp.f...  12.2 us
    reduce_scatter x1, waiting for transfers between devices, shards(): lax.psum_scatter(grad_left_first.astype(jnp.bfloat16), 'dp', scatter_dime...  9.99 us
    reduce_scatter x1, waiting for transfers between devices, shards(): lax.psum_scatter(grad_right_mix.astype(jnp.bfloat16), 'dp', scatter_dimen...  9.97 us
  transfers between devices with their start and end apart: 12, of which 10 were waited for; matrix products, arithmetic and copies ran while one was open for 20% of the time, Pallas kernels for 0%

commit v1 on v0

--- a/solution.py
+++ b/solution.py
@@ -1,7 +1,15 @@
+import functools
+
 import jax
 import jax.numpy as jnp
 from jax import lax
+from jax.experimental import pallas as pl
+from jax.experimental.pallas import tpu as pltpu
 from jax.sharding import PartitionSpec as P
+
+F32 = jnp.float32
+BF16 = jnp.bfloat16
+CHUNKS = 2
 
 
 def outgoing(weight, values, groups):
@@ -126,9 +134,264 @@
     )
 
 
+def mm(a, b):
+    return lax.dot_general(a, b, (((1,), (0,)), ((), ())), preferred_element_type=F32)
+
+
+def mm_nt(a, b):
+    return lax.dot_general(a, b, (((1,), (1,)), ((), ())), preferred_element_type=F32)
+
+
+def fused_kernel(
+    groups, nb, bs, jn, kn, chunks,
+    in_ref, go_ref, rf_ref, lf_ref, rg_ref, lg_ref, rm_ref, lm_ref,
+    out_ref, gin_ref, grf_ref, glf_ref, grg_ref, glg_ref, grm_ref, glm_ref,
+    send_a, recv_a, send_b, recv_b, right_w, right_t, left_w, left_t, wide, gram_r, gram_l,
+    right_send, right_recv, left_send, left_recv,
+    send_sems, recv_sems, pair_send, pair_recv,
+):
+    me = lax.axis_index("block")
+    dp = lax.axis_index("dp")
+    other = 1 - dp
+    rows, count = in_ref.shape
+    tc = count // chunks
+    piece = nb * jn
+
+    barrier = pltpu.get_barrier_semaphore()
+
+    @pl.loop(1, groups)
+    def _(r):
+        pl.semaphore_signal(barrier, inc=1, device_id={"block": lax.rem(me + r, groups)},
+                            device_id_type=pl.DeviceIdType.MESH)
+
+    pl.semaphore_signal(barrier, inc=1, device_id={"dp": other}, device_id_type=pl.DeviceIdType.MESH)
+
+    def expand_right(m, ref):
+        wide[...] = jnp.zeros_like(wide)
+        for b in range(nb):
+            wide[:, b, :, b * bs:(b + 1) * bs] = ref[b].astype(F32).reshape(groups, jn, bs)
+        full = wide[...].reshape(rows, rows)
+        right_w[m] = full.astype(BF16)
+        right_t[m] = full.T.astype(BF16)
+
+    spread = (
+        lax.broadcasted_iota(jnp.int32, (rows, kn), 0) // jn
+        == lax.broadcasted_iota(jnp.int32, (rows, kn), 1)
+    ).astype(F32).astype(BF16)
+    keep = (
+        lax.broadcasted_iota(jnp.int32, (rows, rows), 0) // kn
+        == lax.broadcasted_iota(jnp.int32, (rows, rows), 1) % jn
+    )
+    keep_t = (
+        lax.broadcasted_iota(jnp.int32, (rows, rows), 0) % jn
+        == lax.broadcasted_iota(jnp.int32, (rows, rows), 1) // kn
+    )
+
+    def expand_left(m, ref):
+        flat = ref[...].reshape(rows, kn)
+        left_w[m] = jnp.where(keep, mm_nt(flat, spread), 0.0).astype(BF16)
+        left_t[m] = jnp.where(keep_t, mm_nt(spread, flat), 0.0).astype(BF16)
+
+    def copy_to(phase, src, dst, c, r):
+        peer = lax.rem(me + r, groups)
+        return pltpu.make_async_remote_copy(
+            src_ref=src.at[c, peer], dst_ref=dst.at[c, me],
+            send_sem=send_sems.at[phase, c, r], recv_sem=recv_sems.at[phase, c, r],
+            device_id={"block": peer}, device_id_type=pl.DeviceIdType.MESH,
+        )
+
+    def copy_from(phase, src, dst, c, r):
+        peer = lax.rem(me + groups - r, groups)
+        return pltpu.make_async_remote_copy(
+            src_ref=src.at[c, peer], dst_ref=dst.at[c, peer],
+            send_sem=send_sems.at[phase, c, r], recv_sem=recv_sems.at[phase, c, r],
+            device_id={"block": peer}, device_id_type=pl.DeviceIdType.MESH,
+        )
+
+    def send(phase, src, dst, c):
+        @pl.loop(1, groups)
+        def _(r):
+            copy_to(phase, src, dst, c, r).start()
+
+        dst[c, me] = src[c, me]
+
+    def receive(phase, src, dst, c):
+        @pl.loop(1, groups)
+        def _(r):
+            copy_from(phase, src, dst, c, r).wait_recv()
+
+    def columns(c):
+        return pl.ds(pl.multiple_of(c * tc, tc), tc)
+
+    def put(ref, c, m, result):
+        ref[c, :, m] = result.astype(BF16).reshape(groups, piece, tc)
+
+    def take(ref, c, m):
+        return ref[c, :, m].reshape(rows, tc)
+
+    expand_right(0, rf_ref)
+    expand_right(1, rg_ref)
+    expand_left(2, lm_ref)
+
+    pl.semaphore_wait(barrier, groups)
+
+    @pl.loop(0, chunks)
+    def _(c):
+        v = in_ref[:, columns(c)]
+        put(send_a, c, 0, mm(right_w[0], v))
+        put(send_a, c, 1, mm(right_w[1], v))
+        put(send_a, c, 2, mm(left_t[2], go_ref[:, columns(c)]))
+        send(0, send_a, recv_a, c)
+
+    expand_right(2, rm_ref)
+    expand_left(0, lf_ref)
+    expand_left(1, lg_ref)
+    gram_r[...] = jnp.zeros_like(gram_r)
+    gram_l[...] = jnp.zeros_like(gram_l)
+
+    @pl.loop(0, chunks)
+    def _(c):
+        receive(0, send_a, recv_a, c)
+        first = take(recv_a, c, 0)
+        gated = take(recv_a, c, 1)
+        back = take(recv_a, c, 2)
+        value = mm(left_w[0], first)
+        gate = mm(left_w[1], gated)
+        sigma = 1.0 / (1.0 + jnp.exp(-gate))
+        silu = gate * sigma
+        hidden = (value * silu).astype(BF16)
+        put(send_b, c, 0, mm(right_w[2], hidden))
+        grad_hidden = mm(right_t[2], back)
+        grad_value = (grad_hidden * silu).astype(BF16)
+        grad_gate = (grad_hidden * value * sigma * (1.0 + gate * (1.0 - sigma))).astype(BF16)
+        put(send_b, c, 1, mm(left_t[0], grad_value))
+        put(send_b, c, 2, mm(left_t[1], grad_gate))
+        send(1, send_b, recv_b, c)
+        gram_r[2] += mm_nt(back, hidden)
+        gram_l[0] += mm_nt(grad_value, first)
+        gram_l[1] += mm_nt(grad_gate, gated)
+
+    half = bs // 2
+    khalf = kn // 2
+
+    def pick_right(m):
+        full = gram_r[m].reshape(groups, nb, jn, rows)
+        for b in range(nb):
+            block = full[:, b, :, b * bs:(b + 1) * bs].reshape(2, half, bs)
+            right_send[0, m, b] = block[0].astype(BF16)
+            right_send[1, m, b] = block[1].astype(BF16)
+
+    def pick_left(m):
+        masked = jnp.where(keep, gram_l[m], 0.0).astype(BF16)
+        picked = mm(masked, spread).reshape(jn, 2, khalf, kn)
+        left_send[0, m] = picked[:, 0].astype(BF16)
+        left_send[1, m] = picked[:, 1].astype(BF16)
+
+    pick_right(2)
+    pick_left(0)
+    pick_left(1)
+
+    @pl.loop(0, chunks)
+    def _(c):
+        receive(1, send_b, recv_b, c)
+        mixed = take(recv_b, c, 0)
+        back_first = take(recv_b, c, 1)
+        back_gate = take(recv_b, c, 2)
+        v = in_ref[:, columns(c)]
+        g = go_ref[:, columns(c)]
+        gram_l[2] += mm_nt(g, mixed)
+        gram_r[0] += mm_nt(back_first, v)
+        gram_r[1] += mm_nt(back_gate, v)
+        out_ref[:, columns(c)] = (v.astype(F32) + mm(left_w[2], mixed)).astype(BF16)
+        through = mm(right_t[0], back_first) + mm(right_t[1], back_gate)
+        gin_ref[:, columns(c)] = (g.astype(F32) + through).astype(BF16)
+
+    pick_left(2)
+    pick_right(0)
+    pick_right(1)
+
+    pair = {"dp": other}
+    swap_right = pltpu.make_async_remote_copy(
+        src_ref=right_send.at[other], dst_ref=right_recv, send_sem=pair_send.at[0], recv_sem=pair_recv.at[0],
+        device_id=pair, device_id_type=pl.DeviceIdType.MESH,
+    )
+    swap_left = pltpu.make_async_remote_copy(
+        src_ref=left_send.at[other], dst_ref=left_recv, send_sem=pair_send.at[1], recv_sem=pair_recv.at[1],
+        device_id=pair, device_id_type=pl.DeviceIdType.MESH,
+    )
+    swap_right.start()
+    swap_left.start()
+
+    @pl.loop(0, chunks)
+    def _(c):
+        @pl.loop(1, groups)
+        def _(r):
+            copy_to(0, send_a, recv_a, c, r).wait_send()
+            copy_to(1, send_b, recv_b, c, r).wait_send()
+
+    swap_right.wait()
+    swap_left.wait()
+    for m, ref in enumerate((grf_ref, grg_ref, grm_ref)):
+        ref[...] = right_send[dp, m].astype(F32) + right_recv[m].astype(F32)
+    for m, ref in enumerate((glf_ref, glg_ref, glm_ref)):
+        ref[...] = left_send[dp, m].astype(F32) + left_recv[m].astype(F32)
+
+
+def fused(inputs, grad_out, right_first, left_first, right_gate, left_gate, right_mix, left_mix):
+    groups = lax.axis_size("block")
+    rows, count = inputs.shape
+    nb, bs, _ = right_first.shape
+    jn, kn, _ = left_first.shape
+    chunks = CHUNKS
+    tc = count // chunks
+    piece = nb * jn
+    right_out = jax.ShapeDtypeStruct((nb, bs // 2, bs), F32)
+    left_out = jax.ShapeDtypeStruct((jn, kn // 2, kn), F32)
+    vmem = pl.BlockSpec(memory_space=pltpu.VMEM)
+    moving = pltpu.VMEM((chunks, groups, 3, piece, tc), BF16)
+    factor = pltpu.VMEM((3, rows, rows), BF16)
+    return pl.pallas_call(
+        functools.partial(fused_kernel, groups, nb, bs, jn, kn, chunks),
+        out_shape=(
+            jax.ShapeDtypeStruct(inputs.shape, BF16), jax.ShapeDtypeStruct(inputs.shape, BF16),
+            right_out, left_out, right_out, left_out, right_out, left_out,
+        ),
+        in_specs=[vmem] * 8,
+        out_specs=(vmem,) * 8,
+        scratch_shapes=[
+            moving, moving, moving, moving, factor, factor, factor, factor,
+            pltpu.VMEM((groups, nb, jn, rows), F32),
+            pltpu.VMEM((3, rows, rows), F32),
+            pltpu.VMEM((3, rows, rows), F32),
+            pltpu.VMEM((2, 3, nb, bs // 2, bs), BF16),
+            pltpu.VMEM((3, nb, bs // 2, bs), BF16),
+            pltpu.VMEM((2, 3, jn, kn // 2, kn), BF16),
+            pltpu.VMEM((3, jn, kn // 2, kn), BF16),
+            pltpu.SemaphoreType.DMA((2, chunks, groups)),
+            pltpu.SemaphoreType.DMA((2, chunks, groups)),
+            pltpu.SemaphoreType.DMA((2,)),
+            pltpu.SemaphoreType.DMA((2,)),
+        ],
+        compiler_params=pltpu.CompilerParams(
+            collective_id=0, has_side_effects=True, vmem_limit_bytes=60 * 1024 * 1024
+        ),
+    )(inputs, grad_out, right_first, left_first, right_gate, left_gate, right_mix, left_mix)
+
+
+def layer(*args):
+    groups, pairs = lax.axis_size("block"), lax.axis_size("dp")
+    inputs, right, left = args[0], args[2], args[3]
+    piece = right.shape[0] * left.shape[0]
+    fits = (
+        pairs == 2 and piece % 16 == 0 and left.shape[0] % 8 == 0 and right.shape[1] % 128 == 0
+        and inputs.shape[1] % (128 * CHUNKS) == 0 and groups * piece == inputs.shape[0]
+    )
+    return fused(*args) if fits else shards(*args)
+
+
 def solution(mesh):
     return jax.shard_map(
-        shards,
+        layer,
         mesh=mesh,
         in_specs=(
             P("block", "dp"),

time: 256 us -> 162 us (0.63)
  Pallas kernels: 0 us -> 152 us
  waiting for transfers between devices: 141 us -> 0 us
  matrix products: 38.6 us -> 0 us
  starting transfers between devices: 31.9 us -> 0 us
  between operations: 14.3 us -> 0.66 us
  other arithmetic: 10.4 us -> 0 us
  local copies, waits for them, and re-layouts: 17.6 us -> 8.78 us
    pallas_call x0 -> x1, Pallas kernels: none -> 152 us  [fused(): pl.pallas_call(functools.partial(fused_kernel, groups, nb, bs, jn, kn, ch...]
    all_to_all x6 -> x0, waiting for transfers between devices: 101 us -> none  [the longest x1 22.4 us: shards(): lax.all_to_all(back_mix, 'block', split_axis=1, concat_axis=1, tiled=True)]
    reduce_scatter x6 -> x0, waiting for transfers between devices: 40.4 us -> none  [the longest x1 9.99 us: shards(): lax.psum_scatter(grad_left_first.astype(jnp.bfloat16), 'dp', scatter_dime...]
    dot_general x18 -> x0, matrix products: 38.6 us -> none  [the longest x3 12.2 us: combine(): jnp.einsum('jks,sjt->jkt', weight, arranged, preferred_element_type=jnp.f...]
    all_to_all x6 -> x0, starting transfers between devices: 31.4 us -> none  [the longest x1 6.58 us: shards(): lax.all_to_all(back_mix, 'block', split_axis=1, concat_axis=1, tiled=True)]
    convert_element_type x7 -> x0, other arithmetic: 10.4 us -> none  [the longest x5 7.52 us: shards(): summed_right_first, summed_left_first, summed_right_gate, summed_left_gat...]
    convert_element_type x4 -> x0, local copies, waits for them, and re-layouts: 7.08 us -> none  [the longest x3 5.4 us: left_grads(): return (grad_weight, back_rows.astype(jnp.bfloat16))]
    reshape x3 -> x0, local copies, waits for them, and re-layouts: 3.19 us -> none  [outgoing(): return sectioned.reshape(sectioned.shape[0], groups, -1, sectioned.shape[2])]
  transfers between devices with their start and end apart: 12 -> 0, of which waited for: 10 -> 0; matrix products, arithmetic and copies ran while one was open for 20% -> 0% of each run, Pallas kernels for 0% -> 0%
where the time goes in v1:
time: 162 us
  Pallas kernels  152 us (94%)
  local copies, waits for them, and re-layouts  8.78 us (5%)
    pallas_call x1, Pallas kernels, fused(): pl.pallas_call(functools.partial(fused_kernel, groups, nb, bs, jn, kn, ch...  152 us
    unnamed x22, local copies, waits for them, and re-layouts  8.78 us

profile of v1, /device:TPU:15, one launch (start us, length us, event | category | flops | bytes accessed | tf_op | source)
XLA Modules:
  0.0 161.9 jit_solution(6416010586617064913)
XLA Ops:
  0.6 152.5 %shard_map.143 = (bf16[512,1024]{1,0:T(8,128)(2,1)}, bf16[512,1024]{1,0:T(8,128)(2,1)}, f32[4,64,128]{2,1,0:T(8,128)}, f32[8,32,64]{2,1,0:T(8,128)}, f32[4,64,12...) custom-call(bf16[512,1024]{1,0:T(8,128)(2,1)} %in_ref.1, ...), custom_call_target="tpu_custom_call" | custom-call | tf_op jit(solution)/shard_map/pallas_call | solution.py:353
  153.1 0.0 copy-start
  153.1 2.4 %copy.24 = bf16[512,1024]{1,0:T(8,128)(2,1)} copy(bf16[512,1024]{1,0:T(8,128)(2,1)} %get-tuple-element.16) | data formatting | bytes 2097152
  155.5 0.0 copy-done
  155.5 0.0 copy-start.6
  155.5 1.0 copy.25
  156.4 0.1 copy-done.6
  156.5 0.0 copy-start.5
  156.5 0.7 copy.26
  157.2 0.3 copy-done.5
  157.4 0.0 copy-start.4
  157.5 0.7 copy.27
  158.1 0.3 copy-done.4
  158.4 0.0 copy-start.3
  158.4 0.7 copy.28
  159.1 0.3 copy-done.3
  159.4 0.0 copy-start.2
  159.4 0.7 copy.29
  160.0 0.3 copy-done.2
  160.3 0.0 copy-start.1
  160.3 0.7 copy.30
  161.0 0.3 copy-done.1
  161.3 0.7 copy.31
Async XLA Ops:
  153.1 2.4 %copy-start = (bf16[512,1024]{1,0:T(8,128)(2,1)S(1)}, bf16[512,1024]{1,0:T(8,128)(2,1)}, u32[]{:S(2)}) copy-start(bf16[512,1024]{1,0:T(8,128)(2,1)} %get-tuple-element.17) | copy-start | bytes 3145732
  155.5 1.0 copy-start.6
  156.5 1.0 copy-start.5
  157.4 1.0 copy-start.4
  158.4 1.0 copy-start.3
  159.4 1.0 copy-start.2
  160.3 1.0 copy-start.1

commit v2 on v1

--- a/solution.py
+++ b/solution.py
@@ -9,7 +9,7 @@
 
 F32 = jnp.float32
 BF16 = jnp.bfloat16
-CHUNKS = 2
+CHUNKS = 4
 
 
 def outgoing(weight, values, groups):
@@ -145,7 +145,7 @@
 def fused_kernel(
     groups, nb, bs, jn, kn, chunks,
     in_ref, go_ref, rf_ref, lf_ref, rg_ref, lg_ref, rm_ref, lm_ref,
-    out_ref, gin_ref, grf_ref, glf_ref, grg_ref, glg_ref, grm_ref, glm_ref,
+    out_ref, gin_ref, gr_ref, gl_ref,
     send_a, recv_a, send_b, recv_b, right_w, right_t, left_w, left_t, wide, gram_r, gram_l,
     right_send, right_recv, left_send, left_recv,
     send_sems, recv_sems, pair_send, pair_recv,
@@ -172,7 +172,9 @@
             wide[:, b, :, b * bs:(b + 1) * bs] = ref[b].astype(F32).reshape(groups, jn, bs)
         full = wide[...].reshape(rows, rows)
         right_w[m] = full.astype(BF16)
-        right_t[m] = full.T.astype(BF16)
+
+    def turn_right(m):
+        right_t[m] = right_w[m].astype(F32).T.astype(BF16)
 
     spread = (
         lax.broadcasted_iota(jnp.int32, (rows, kn), 0) // jn
@@ -188,9 +190,10 @@
     )
 
     def expand_left(m, ref):
-        flat = ref[...].reshape(rows, kn)
-        left_w[m] = jnp.where(keep, mm_nt(flat, spread), 0.0).astype(BF16)
-        left_t[m] = jnp.where(keep_t, mm_nt(spread, flat), 0.0).astype(BF16)
+        left_w[m] = jnp.where(keep, mm_nt(ref[...].reshape(rows, kn), spread), 0.0).astype(BF16)
+
+    def turn_left(m, ref):
+        left_t[m] = jnp.where(keep_t, mm_nt(spread, ref[...].reshape(rows, kn)), 0.0).astype(BF16)
 
     def copy_to(phase, src, dst, c, r):
         peer = lax.rem(me + r, groups)
@@ -209,8 +212,9 @@
         )
 
     def send(phase, src, dst, c):
-        @pl.loop(1, groups)
-        def _(r):
+        @pl.loop(0, groups - 1)
+        def _(n):
+            r = groups // 2 + (1 - 2 * lax.rem(n, 2)) * ((n + 1) // 2)
             copy_to(phase, src, dst, c, r).start()
 
         dst[c, me] = src[c, me]
@@ -231,7 +235,7 @@
 
     expand_right(0, rf_ref)
     expand_right(1, rg_ref)
-    expand_left(2, lm_ref)
+    turn_left(2, lm_ref)
 
     pl.semaphore_wait(barrier, groups)
 
@@ -243,9 +247,12 @@
         put(send_a, c, 2, mm(left_t[2], go_ref[:, columns(c)]))
         send(0, send_a, recv_a, c)
 
-    expand_right(2, rm_ref)
     expand_left(0, lf_ref)
     expand_left(1, lg_ref)
+    expand_right(2, rm_ref)
+    turn_right(2)
+    turn_left(0, lf_ref)
+    turn_left(1, lg_ref)
     gram_r[...] = jnp.zeros_like(gram_r)
     gram_l[...] = jnp.zeros_like(gram_l)
 
@@ -287,40 +294,55 @@
         left_send[0, m] = picked[:, 0].astype(BF16)
         left_send[1, m] = picked[:, 1].astype(BF16)
 
+    pair = {"dp": other}
+
+    def swap(n, src, dst):
+        return pltpu.make_async_remote_copy(
+            src_ref=src, dst_ref=dst, send_sem=pair_send.at[n], recv_sem=pair_recv.at[n],
+            device_id=pair, device_id_type=pl.DeviceIdType.MESH,
+        )
+
+    swaps = [
+        swap(0, right_send.at[other, 2], right_recv.at[2]),
+        swap(1, left_send.at[other, pl.ds(0, 2)], left_recv.at[pl.ds(0, 2)]),
+        swap(2, right_send.at[other, pl.ds(0, 2)], right_recv.at[pl.ds(0, 2)]),
+        swap(3, left_send.at[other, 2], left_recv.at[2]),
+    ]
     pick_right(2)
     pick_left(0)
     pick_left(1)
-
-    @pl.loop(0, chunks)
-    def _(c):
+    swaps[0].start()
+    swaps[1].start()
+    turn_right(0)
+    turn_right(1)
+    expand_left(2, lm_ref)
+
+    def last_grams(c):
         receive(1, send_b, recv_b, c)
-        mixed = take(recv_b, c, 0)
-        back_first = take(recv_b, c, 1)
-        back_gate = take(recv_b, c, 2)
+        gram_l[2] += mm_nt(go_ref[:, columns(c)], take(recv_b, c, 0))
+        v = in_ref[:, columns(c)]
+        gram_r[0] += mm_nt(take(recv_b, c, 1), v)
+        gram_r[1] += mm_nt(take(recv_b, c, 2), v)
+
+    def last_rows(c):
         v = in_ref[:, columns(c)]
         g = go_ref[:, columns(c)]
-        gram_l[2] += mm_nt(g, mixed)
-        gram_r[0] += mm_nt(back_first, v)
-        gram_r[1] += mm_nt(back_gate, v)
-        out_ref[:, columns(c)] = (v.astype(F32) + mm(left_w[2], mixed)).astype(BF16)
-        through = mm(right_t[0], back_first) + mm(right_t[1], back_gate)
+        out_ref[:, columns(c)] = (v.astype(F32) + mm(left_w[2], take(recv_b, c, 0))).astype(BF16)
+        through = mm(right_t[0], take(recv_b, c, 1)) + mm(right_t[1], take(recv_b, c, 2))
         gin_ref[:, columns(c)] = (g.astype(F32) + through).astype(BF16)
 
+    @pl.loop(0, chunks - 1)
+    def _(c):
+        last_grams(c)
+        last_rows(c)
+
+    last_grams(chunks - 1)
     pick_left(2)
     pick_right(0)
     pick_right(1)
-
-    pair = {"dp": other}
-    swap_right = pltpu.make_async_remote_copy(
-        src_ref=right_send.at[other], dst_ref=right_recv, send_sem=pair_send.at[0], recv_sem=pair_recv.at[0],
-        device_id=pair, device_id_type=pl.DeviceIdType.MESH,
-    )
-    swap_left = pltpu.make_async_remote_copy(
-        src_ref=left_send.at[other], dst_ref=left_recv, send_sem=pair_send.at[1], recv_sem=pair_recv.at[1],
-        device_id=pair, device_id_type=pl.DeviceIdType.MESH,
-    )
-    swap_right.start()
-    swap_left.start()
+    swaps[2].start()
+    swaps[3].start()
+    last_rows(chunks - 1)
 
     @pl.loop(0, chunks)
     def _(c):
@@ -329,12 +351,21 @@
             copy_to(0, send_a, recv_a, c, r).wait_send()
             copy_to(1, send_b, recv_b, c, r).wait_send()
 
-    swap_right.wait()
-    swap_left.wait()
-    for m, ref in enumerate((grf_ref, grg_ref, grm_ref)):
-        ref[...] = right_send[dp, m].astype(F32) + right_recv[m].astype(F32)
-    for m, ref in enumerate((glf_ref, glg_ref, glm_ref)):
-        ref[...] = left_send[dp, m].astype(F32) + left_recv[m].astype(F32)
+    for each in swaps:
+        each.wait()
+    gr_ref[...] = right_send[dp].astype(F32) + right_recv[...].astype(F32)
+    gl_ref[...] = left_send[dp].astype(F32) + left_recv[...].astype(F32)
+
+
+def results_kernel(out_in, gin_in, gr_in, gl_in, out, gin, grf, glf, grg, glg, grm, glm, sems):
+    moves = [(out_in, out), (gin_in, gin)]
+    moves += [(gr_in.at[m], ref) for m, ref in enumerate((grf, grg, grm))]
+    moves += [(gl_in.at[m], ref) for m, ref in enumerate((glf, glg, glm))]
+    copies = [pltpu.make_async_copy(src, dst, sems.at[n]) for n, (src, dst) in enumerate(moves)]
+    for copy in copies:
+        copy.start()
+    for copy in copies:
+        copy.wait()
 
 
 def fused(inputs, grad_out, right_first, left_first, right_gate, left_gate, right_mix, left_mix):
@@ -350,14 +381,14 @@
     vmem = pl.BlockSpec(memory_space=pltpu.VMEM)
     moving = pltpu.VMEM((chunks, groups, 3, piece, tc), BF16)
     factor = pltpu.VMEM((3, rows, rows), BF16)
-    return pl.pallas_call(
+    moved = pl.pallas_call(
         functools.partial(fused_kernel, groups, nb, bs, jn, kn, chunks),
         out_shape=(
             jax.ShapeDtypeStruct(inputs.shape, BF16), jax.ShapeDtypeStruct(inputs.shape, BF16),
-            right_out, left_out, right_out, left_out, right_out, left_out,
+            jax.ShapeDtypeStruct((3,) + right_out.shape, F32), jax.ShapeDtypeStruct((3,) + left_out.shape, F32),
         ),
         in_specs=[vmem] * 8,
-        out_specs=(vmem,) * 8,
+        out_specs=(vmem,) * 4,
         scratch_shapes=[
             moving, moving, moving, moving, factor, factor, factor, factor,
             pltpu.VMEM((groups, nb, jn, rows), F32),
@@ -369,13 +400,24 @@
             pltpu.VMEM((3, jn, kn // 2, kn), BF16),
             pltpu.SemaphoreType.DMA((2, chunks, groups)),
             pltpu.SemaphoreType.DMA((2, chunks, groups)),
-            pltpu.SemaphoreType.DMA((2,)),
-            pltpu.SemaphoreType.DMA((2,)),
+            pltpu.SemaphoreType.DMA((4,)),
+            pltpu.SemaphoreType.DMA((4,)),
         ],
         compiler_params=pltpu.CompilerParams(
             collective_id=0, has_side_effects=True, vmem_limit_bytes=60 * 1024 * 1024
         ),
     )(inputs, grad_out, right_first, left_first, right_gate, left_gate, right_mix, left_mix)
+    anywhere = pl.BlockSpec(memory_space=pl.ANY)
+    return pl.pallas_call(
+        results_kernel,
+        out_shape=(
+            jax.ShapeDtypeStruct(inputs.shape, BF16), jax.ShapeDtypeStruct(inputs.shape, BF16),
+            right_out, left_out, right_out, left_out, right_out, left_out,
+        ),
+        in_specs=[anywhere] * 4,
+        out_specs=(anywhere,) * 8,
+        scratch_shapes=[pltpu.SemaphoreType.DMA((8,))],
+    )(*moved)
 
 
 def layer(*args):

time: 162 us -> 239 us (1.48)
  Pallas kernels: 152 us -> 238 us
  local copies, waits for them, and re-layouts: 8.78 us -> 0 us
    pallas_call x0 -> x1, Pallas kernels: none -> 88.5 us  [fused(): pl.pallas_call(results_kernel, out_shape=(jax.ShapeDtypeStruct(inputs.sha...]
    unnamed x22 -> x0, local copies, waits for them, and re-layouts: 8.78 us -> none
    pallas_call x1, Pallas kernels: 152 us -> 149 us  [fused(): pl.pallas_call(functools.partial(fused_kernel, groups, nb, bs, jn, kn, ch...]
where the time goes in v2:
time: 239 us
  Pallas kernels  238 us (100%)
    pallas_call x1, Pallas kernels, fused(): pl.pallas_call(functools.partial(fused_kernel, groups, nb, bs, jn, kn, ch...  149 us
    pallas_call x1, Pallas kernels, fused(): pl.pallas_call(results_kernel, out_shape=(jax.ShapeDtypeStruct(inputs.sha...  88.5 us

profile of v2, /device:TPU:15, one launch (start us, length us, event | category | flops | bytes accessed | tf_op | source)
XLA Modules:
  0.0 238.6 jit_solution(12040739010523535855)
XLA Ops:
  0.6 149.4 %shard_map.143 = (bf16[512,1024]{1,0:T(8,128)(2,1)}, bf16[512,1024]{1,0:T(8,128)(2,1)}, f32[3,4,64,128]{3,2,1,0:T(8,128)}, f32[3,8,32,64]{3,2,1,0:T(8,128)}) custom-call(bf16[512,1024]{1,0:T(8,128)(2,1)} %in_ref.1, bf16[512,1024]{1,0:T(8,128)(2,1)} %go_ref.1, bf16[4,128,128]{2,1,0:T(8,128)(2,1)} %rf_ref.1, bf16[8,64,64]{2,1,0:T(8,128)(2,1)} %lf_ref.1, ...), custom_call_target="tpu_custom_call" | custom-call | tf_op jit(solution)/shard_map/pallas_call | solution.py:384
  150.0 88.5 %shard_map.144 = (bf16[512,1024]{1,0:T(8,128)(2,1)}, bf16[512,1024]{1,0:T(8,128)(2,1)}, f32[4,64,128]{2,1,0:T(8,128)}, f32[8,32,64]{2,1,0:T(8,128)}, f32[4,64,12...) custom-call(bf16[512,1024]{1,0:T(8,128)(2,1)} %get-tuple-element.12.out_in, ...), custom_call_target="tpu_custom_call" | custom-call | tf_op jit(solution)/shard_map/pallas_call | solution.py:411

commit v3 on v2

--- a/solution.py
+++ b/solution.py
@@ -214,7 +214,7 @@
     def send(phase, src, dst, c):
         @pl.loop(0, groups - 1)
         def _(n):
-            r = groups // 2 + (1 - 2 * lax.rem(n, 2)) * ((n + 1) // 2)
+            r = n + 1
             copy_to(phase, src, dst, c, r).start()
 
         dst[c, me] = src[c, me]
@@ -357,15 +357,21 @@
     gl_ref[...] = left_send[dp].astype(F32) + left_recv[...].astype(F32)
 
 
-def results_kernel(out_in, gin_in, gr_in, gl_in, out, gin, grf, glf, grg, glg, grm, glm, sems):
-    moves = [(out_in, out), (gin_in, gin)]
-    moves += [(gr_in.at[m], ref) for m, ref in enumerate((grf, grg, grm))]
-    moves += [(gl_in.at[m], ref) for m, ref in enumerate((glf, glg, glm))]
-    copies = [pltpu.make_async_copy(src, dst, sems.at[n]) for n, (src, dst) in enumerate(moves)]
-    for copy in copies:
-        copy.start()
-    for copy in copies:
-        copy.wait()
+def results_kernel(
+    out_in, gin_in, gr_in, gl_in, out, gin, grf, glf, grg, glg, grm, glm, rows_held, right_held, left_held, in_sems, out_sems
+):
+    steps = [(out_in, rows_held.at[0], out), (gin_in, rows_held.at[1], gin)]
+    steps += [(gr_in.at[m], right_held.at[m], ref) for m, ref in enumerate((grf, grg, grm))]
+    steps += [(gl_in.at[m], left_held.at[m], ref) for m, ref in enumerate((glf, glg, glm))]
+    loads = [pltpu.make_async_copy(src, held, in_sems.at[n]) for n, (src, held, _) in enumerate(steps)]
+    stores = [pltpu.make_async_copy(held, dst, out_sems.at[n]) for n, (_, held, dst) in enumerate(steps)]
+    for load in loads:
+        load.start()
+    for load, store in zip(loads, stores):
+        load.wait()
+        store.start()
+    for store in stores:
+        store.wait()
 
 
 def fused(inputs, grad_out, right_first, left_first, right_gate, left_gate, right_mix, left_mix):
@@ -416,7 +422,13 @@
         ),
         in_specs=[anywhere] * 4,
         out_specs=(anywhere,) * 8,
-        scratch_shapes=[pltpu.SemaphoreType.DMA((8,))],
+        scratch_shapes=[
+            pltpu.VMEM((2,) + inputs.shape, BF16),
+            pltpu.VMEM((3,) + right_out.shape, F32),
+            pltpu.VMEM((3,) + left_out.shape, F32),
+            pltpu.SemaphoreType.DMA((8,)),
+            pltpu.SemaphoreType.DMA((8,)),
+        ],
     )(*moved)
 
 

time: 239 us -> 153 us (0.64)
  Pallas kernels: 238 us -> 152 us
    pallas_call x1, Pallas kernels: 88.5 us -> 2.93 us  [fused(): pl.pallas_call(results_kernel, out_shape=(jax.ShapeDtypeStruct(inputs.sha...]
where the time goes in v3:
time: 153 us
  Pallas kernels  152 us (99%)
    pallas_call x1, Pallas kernels, fused(): pl.pallas_call(functools.partial(fused_kernel, groups, nb, bs, jn, kn, ch...  149 us

profile of v3, /device:TPU:15, one launch (start us, length us, event | category | flops | bytes accessed | tf_op | source)
XLA Modules:
  0.0 153.0 jit_solution(6138562520060431594)
XLA Ops:
  0.6 149.4 %shard_map.143 = (bf16[512,1024]{1,0:T(8,128)(2,1)}, bf16[512,1024]{1,0:T(8,128)(2,1)}, f32[3,4,64,128]{3,2,1,0:T(8,128)}, f32[3,8,32,64]{3,2,1,0:T(8,128)}) custom-call(bf16[512,1024]{1,0:T(8,128)(2,1)} %in_ref.1, bf16[512,1024]{1,0:T(8,128)(2,1)} %go_ref.1, bf16[4,128,128]{2,1,0:T(8,128)(2,1)} %rf_ref.1, bf16[8,64,64]{2,1,0:T(8,128)(2,1)} %lf_ref.1, ...), custom_call_target="tpu_custom_call" | custom-call | tf_op jit(solution)/shard_map/pallas_call | solution.py:390
  150.1 2.9 %shard_map.144 = (bf16[512,1024]{1,0:T(8,128)(2,1)}, bf16[512,1024]{1,0:T(8,128)(2,1)}, f32[4,64,128]{2,1,0:T(8,128)}, f32[8,32,64]{2,1,0:T(8,128)}, f32[4,64,12...) custom-call(bf16[512,1024]{1,0:T(8,128)(2,1)} %get-tuple-element.12.out_in, ...), custom_call_target="tpu_custom_call" | custom-call | tf_op jit(solution)/shard_map/pallas_call | solution.py:417

commit v4 on v3

--- a/solution.py
+++ b/solution.py
@@ -211,6 +211,15 @@
             device_id={"block": peer}, device_id_type=pl.DeviceIdType.MESH,
         )
 
+    def pair_copy(p, r, incoming):
+        peer = lax.rem(me + groups - r, groups) if incoming else lax.rem(me + r, groups)
+        return pltpu.make_async_remote_copy(
+            src_ref=send_a.at[pl.ds(2 * p, 2), peer],
+            dst_ref=recv_a.at[pl.ds(2 * p, 2), peer if incoming else me],
+            send_sem=send_sems.at[0, p, r], recv_sem=recv_sems.at[0, p, r],
+            device_id={"block": peer}, device_id_type=pl.DeviceIdType.MESH,
+        )
+
     def send(phase, src, dst, c):
         @pl.loop(0, groups - 1)
         def _(n):
@@ -239,13 +248,19 @@
 
     pl.semaphore_wait(barrier, groups)
 
-    @pl.loop(0, chunks)
-    def _(c):
-        v = in_ref[:, columns(c)]
-        put(send_a, c, 0, mm(right_w[0], v))
-        put(send_a, c, 1, mm(right_w[1], v))
-        put(send_a, c, 2, mm(left_t[2], go_ref[:, columns(c)]))
-        send(0, send_a, recv_a, c)
+    @pl.loop(0, chunks // 2)
+    def _(p):
+        for n in range(2):
+            c = 2 * p + n
+            v = in_ref[:, columns(c)]
+            put(send_a, c, 0, mm(right_w[0], v))
+            put(send_a, c, 1, mm(right_w[1], v))
+            put(send_a, c, 2, mm(left_t[2], go_ref[:, columns(c)]))
+            recv_a[c, me] = send_a[c, me]
+
+        @pl.loop(1, groups)
+        def _(r):
+            pair_copy(p, r, False).start()
 
     expand_left(0, lf_ref)
     expand_left(1, lg_ref)
@@ -258,7 +273,12 @@
 
     @pl.loop(0, chunks)
     def _(c):
-        receive(0, send_a, recv_a, c)
+        @pl.when(lax.rem(c, 2) == 0)
+        def _():
+            @pl.loop(1, groups)
+            def _(r):
+                pair_copy(c // 2, r, True).wait_recv()
+
         first = take(recv_a, c, 0)
         gated = take(recv_a, c, 1)
         back = take(recv_a, c, 2)
@@ -344,11 +364,14 @@
     swaps[3].start()
     last_rows(chunks - 1)
 
-    @pl.loop(0, chunks)
-    def _(c):
-        @pl.loop(1, groups)
-        def _(r):
-            copy_to(0, send_a, recv_a, c, r).wait_send()
+    @pl.loop(1, groups)
+    def _(r):
+        @pl.loop(0, chunks // 2)
+        def _(p):
+            pair_copy(p, r, False).wait_send()
+
+        @pl.loop(0, chunks)
+        def _(c):
             copy_to(1, send_b, recv_b, c, r).wait_send()
 
     for each in swaps:

time: 153 us -> 155 us (1.013)
  Pallas kernels: 152 us -> 155 us
    pallas_call x1, Pallas kernels: 149 us -> 152 us  [fused(): pl.pallas_call(functools.partial(fused_kernel, groups, nb, bs, jn, kn, ch...]
where the time goes in v4:
time: 155 us
  Pallas kernels  155 us (100%)
    pallas_call x1, Pallas kernels, fused(): pl.pallas_call(functools.partial(fused_kernel, groups, nb, bs, jn, kn, ch...  152 us

profile of v4, /device:TPU:15, one launch (start us, length us, event | category | flops | bytes accessed | tf_op | source)
XLA Modules:
  0.0 155.3 jit_solution(12166555134889136202)
XLA Ops:
  0.6 151.7 %shard_map.143 = (bf16[512,1024]{1,0:T(8,128)(2,1)}, bf16[512,1024]{1,0:T(8,128)(2,1)}, f32[3,4,64,128]{3,2,1,0:T(8,128)}, f32[3,8,32,64]{3,2,1,0:T(8,128)}) custom-call(bf16[512,1024]{1,0:T(8,128)(2,1)} %in_ref.1, bf16[512,1024]{1,0:T(8,128)(2,1)} %go_ref.1, bf16[4,128,128]{2,1,0:T(8,128)(2,1)} %rf_ref.1, bf16[8,64,64]{2,1,0:T(8,128)(2,1)} %lf_ref.1, ...), custom_call_target="tpu_custom_call" | custom-call | tf_op jit(solution)/shard_map/pallas_call | solution.py:413
  152.4 2.9 %shard_map.144 = (bf16[512,1024]{1,0:T(8,128)(2,1)}, bf16[512,1024]{1,0:T(8,128)(2,1)}, f32[4,64,128]{2,1,0:T(8,128)}, f32[8,32,64]{2,1,0:T(8,128)}, f32[4,64,12...) custom-call(bf16[512,1024]{1,0:T(8,128)(2,1)} %get-tuple-element.12.out_in, ...), custom_call_target="tpu_custom_call" | custom-call | tf_op jit(solution)/shard_map/pallas_call | solution.py:440

commit v5 on v3

--- a/solution.py
+++ b/solution.py
@@ -360,7 +360,12 @@
 def results_kernel(
     out_in, gin_in, gr_in, gl_in, out, gin, grf, glf, grg, glg, grm, glm, rows_held, right_held, left_held, in_sems, out_sems
 ):
-    steps = [(out_in, rows_held.at[0], out), (gin_in, rows_held.at[1], gin)]
+    quarter = out.shape[0] // 4
+    steps = []
+    for q in range(4):
+        part = pl.ds(q * quarter, quarter)
+        steps.append((out_in.at[part], rows_held.at[0, part], out.at[part]))
+        steps.append((gin_in.at[part], rows_held.at[1, part], gin.at[part]))
     steps += [(gr_in.at[m], right_held.at[m], ref) for m, ref in enumerate((grf, grg, grm))]
     steps += [(gl_in.at[m], left_held.at[m], ref) for m, ref in enumerate((glf, glg, glm))]
     loads = [pltpu.make_async_copy(src, held, in_sems.at[n]) for n, (src, held, _) in enumerate(steps)]
@@ -426,8 +431,8 @@
             pltpu.VMEM((2,) + inputs.shape, BF16),
             pltpu.VMEM((3,) + right_out.shape, F32),
             pltpu.VMEM((3,) + left_out.shape, F32),
-            pltpu.SemaphoreType.DMA((8,)),
-            pltpu.SemaphoreType.DMA((8,)),
+            pltpu.SemaphoreType.DMA((14,)),
+            pltpu.SemaphoreType.DMA((14,)),
         ],
     )(*moved)
 

time: 153 us -> 153 us (level)
  no operation moved by 1% of the time
where the time goes in v5:
time: 153 us
  Pallas kernels  152 us (99%)
    pallas_call x1, Pallas kernels, fused(): pl.pallas_call(functools.partial(fused_kernel, groups, nb, bs, jn, kn, ch...  149 us

profile of v5, /device:TPU:15, one launch (start us, length us, event | category | flops | bytes accessed | tf_op | source)
XLA Modules:
  0.0 152.8 jit_solution(13620403675589629868)
XLA Ops:
  0.6 149.4 %shard_map.143 = (bf16[512,1024]{1,0:T(8,128)(2,1)}, bf16[512,1024]{1,0:T(8,128)(2,1)}, f32[3,4,64,128]{3,2,1,0:T(8,128)}, f32[3,8,32,64]{3,2,1,0:T(8,128)}) custom-call(bf16[512,1024]{1,0:T(8,128)(2,1)} %in_ref.1, bf16[512,1024]{1,0:T(8,128)(2,1)} %go_ref.1, bf16[4,128,128]{2,1,0:T(8,128)(2,1)} %rf_ref.1, bf16[8,64,64]{2,1,0:T(8,128)(2,1)} %lf_ref.1, ...), custom_call_target="tpu_custom_call" | custom-call | tf_op jit(solution)/shard_map/pallas_call | solution.py:395
  150.1 2.8 %shard_map.144 = (bf16[512,1024]{1,0:T(8,128)(2,1)}, bf16[512,1024]{1,0:T(8,128)(2,1)}, f32[4,64,128]{2,1,0:T(8,128)}, f32[8,32,64]{2,1,0:T(8,128)}, f32[4,64,12...) custom-call(bf16[512,1024]{1,0:T(8,128)(2,1)} %get-tuple-element.12.out_in, ...), custom_call_target="tpu_custom_call" | custom-call | tf_op jit(solution)/shard_map/pallas_call | solution.py:422
